TPU v7x, 128 devices: a whole 4x4x4 slice. The times are simulated.
128 devices in a mesh: slab: 8 (over z, core), leaf: 16 (over y, x).
Axes of the slice: x: 4, y: 4, z: 4, core: 2. Of those that a mesh axis runs over, the one named last changes fastest.
Arguments:
- sources: float32 [8, 16, 512, 1024], P('slab', 'leaf'), may hold values from -6 to 6
- merge_ops: float32 [4, 8, 16, 512, 1024], P(None, 'slab', 'leaf'), may hold values from -1 to 1
- sweep_ops: float32 [8, 16, 512, 512], P('slab', 'leaf'), may hold values from -1 to 1
Outputs:
- interface: float32 [8, 16, 512, 1024], P('slab', 'leaf')
All inputs are finite; a program needn't handle non-finite values.
Results may differ from a plain program's by a relative error of at most 0.00017.
Values sent between devices are 32-bit elements; how exact they have to be, the bound alone decides.
A program may use at most 64 MiB of HBM per device.

v0:
```python
import jax
import jax.numpy as jnp
from jax import lax
from jax.sharding import PartitionSpec as P


def partner_2(block, axis, apart):
    count = lax.axis_size(axis)
    route = []
    for low in range(count):
        high = low | 1 << apart
        if high != low and high < count:
            route += [(low, high), (high, low)]
    return lax.ppermute(block, axis, route)


def shifted(value, axis, by):
    length = lax.axis_size(axis)
    pairs = [(i, i + by) for i in range(length) if 0 <= i + by < length]
    return lax.ppermute(value, axis, pairs)


def product(left, right):
    return jnp.dot(left, right, preferred_element_type=jnp.float32, precision=lax.Precision.HIGHEST)


def per_device(sources, merge_ops, sweep_ops):
    current = sources[0, 0]
    merge_local = merge_ops[:, 0, 0]
    height = current.shape[0]
    leaf_bits = lax.axis_size("leaf").bit_length() - 1
    for level_index in range(merge_local.shape[0]):
        partner = partner_2(current, "leaf", level_index % leaf_bits)
        current = product(merge_local[level_index, :, :height], current) + product(
            merge_local[level_index, :, height:], partner
        )
    sweep_local = sweep_ops[0, 0]

    def advance(step, carried):
        received = shifted(carried, "slab", 1)
        return product(sweep_local, received + current)

    carried = product(sweep_local, current)
    carried = lax.fori_loop(0, lax.axis_size("slab") - 1, advance, carried)
    return carried[None, None]


def solution(mesh):
    in_specs = (
        P("slab", "leaf", None, None),
        P(None, "slab", "leaf", None, None),
        P("slab", "leaf", None, None),
    )
    out_specs = P("slab", "leaf", None, None)
    return jax.shard_map(
        per_device, mesh=mesh, in_specs=in_specs, out_specs=out_specs, check_vma=False
    )
```

profile of v0, /device:TPU:96, one launch (start us, length us, event | category | flops | bytes accessed | tf_op | source)
XLA Modules:
  0.0 455.7 jit_solution(11664917396628971115)
XLA Ops:
  1.5 5.6 %fusion.8 = f32[512,1024]{1,0:T(8,128)S(1)} fusion(f32[4,512,1024]{2,1,0:T(8,128)} %bitcast.54, f32[1,1,512,1024]{3,2,1,0:T(8,128)} %param.5), kind=kOutput, calls=%fused_computation.19 | convolution fusion | flops 3221225472 | bytes 5242880 | tf_op jit(solution)/shard_map/dot_general | solution.py:24
  7.1 40.5 %collective-permute-done.1 = f32[512,1024]{1,0:T(8,128)S(1)} collective-permute-done((f32[512,1024]{1,0:T(8,128)}, f32[512,1024]{1,0:T(8,128)S(1)}, u32[]{:S(2)}, u32[]{:S(2)}) %collective-permute-start.1) | collective-permute-done | bytes 2097184 | tf_op jit(solution)/shard_map/ppermute | solution.py:14
  47.6 4.8 %convolution_add_fusion.3 = f32[512,1024]{1,0:T(8,128)S(1)} fusion(f32[512,1024]{1,0:T(8,128)S(1)} %fusion.8, f32[512,1024]{1,0:T(8,128)S(1)} %collective-permute-done.1, f32[4,512,1024]{2,1,0:T(8,128)} %bitcast.55), kind=kOutput, calls=%fused_computation.7 | convolution fusion | flops 3221749760 | bytes 7340032 | tf_op jit(solution)/shard_map/dot_general | solution.py:24
  52.4 3.3 collective-permute-start.2
  55.7 6.9 %fusion.7 = f32[1024,512]{1,0:T(8,128)S(1)} fusion(f32[512,1024]{1,0:T(8,128)S(1)} %convolution_add_fusion.3, f32[4,512,1024]{2,1,0:T(8,128)S(1)} %bitcast.58), kind=kOutput, calls=%fused_computation.16 | convolution fusion | flops 3221225472 | bytes 5242880 | tf_op jit(solution)/shard_map/dot_general | solution.py:24
  62.6 38.1 %collective-permute-done.2 = f32[512,1024]{1,0:T(8,128)S(1)} collective-permute-done((f32[512,1024]{1,0:T(8,128)S(1)}, f32[512,1024]{1,0:T(8,128)S(1)}, u32[]{:S(2)}, u32[]{:S(2)}) %collective-permute-start.2) | collective-permute-done | bytes 2097184 | tf_op jit(solution)/shard_map/ppermute | solution.py:14
  100.7 7.1 %convolution_add_fusion.2 = f32[1024,512]{1,0:T(8,128)S(1)} fusion(f32[1024,512]{1,0:T(8,128)S(1)} %fusion.7, f32[512,1024]{1,0:T(8,128)S(1)} %collective-permute-done.2, f32[4,512,1024]{2,1,0:T(8,128)S(1)} %bitcast.59), kind=kOutput, calls=%fused_computation.6 | convolution fusion | flops 3221749760 | bytes 7340032 | tf_op jit(solution)/shard_map/dot_general | solution.py:24
  109.4 3.5 fusion.6
  112.9 40.5 %collective-permute-done.3 = f32[512,1024]{0,1:T(8,128)S(1)} collective-permute-done((f32[512,1024]{0,1:T(8,128)S(1)}, f32[512,1024]{0,1:T(8,128)S(1)}, u32[]{:S(2)}, u32[]{:S(2)}) %collective-permute-start.3) | collective-permute-done | bytes 2097184 | tf_op jit(solution)/shard_map/ppermute | solution.py:14
  153.4 3.6 convolution_add_fusion.1
  157.0 3.5 collective-permute-start.4
  160.5 4.7 %fusion.5 = f32[1024,512]{1,0:T(8,128)S(1)} fusion(f32[1024,512]{1,0:T(8,128)S(1)} %convolution_add_fusion.1, f32[4,512,1024]{2,1,0:T(8,128)} %bitcast.56), kind=kOutput, calls=%fused_computation.10 | convolution fusion | flops 3221225472 | bytes 5242880 | tf_op jit(solution)/shard_map/dot_general | solution.py:24
  165.2 38.4 %collective-permute-done.4 = f32[512,1024]{0,1:T(8,128)} collective-permute-done((f32[512,1024]{0,1:T(8,128)S(1)}, f32[512,1024]{0,1:T(8,128)}, u32[]{:S(2)}, u32[]{:S(2)}) %collective-permute-start.4) | collective-permute-done | bytes 2097184 | tf_op jit(solution)/shard_map/ppermute | solution.py:14
  203.6 5.4 %convolution_add_fusion = f32[1024,512]{1,0:T(8,128)S(1)} fusion(f32[1024,512]{1,0:T(8,128)S(1)} %fusion.5, f32[512,1024]{0,1:T(8,128)} %collective-permute-done.4, f32[4,512,1024]{2,1,0:T(8,128)} %bitcast.57), kind=kOutput, calls=%fused_computation.4 | convolution fusion | flops 3221749760 | bytes 7340032 | tf_op jit(solution)/shard_map/dot_general | solution.py:24
  209.0 4.8 %convolution_bitcast_fusion = f32[512,1024]{0,1:T(8,128)} fusion(f32[1024,512]{1,0:T(8,128)S(1)} %convolution_add_fusion, f32[1,1,512,512]{3,2,1,0:T(8,128)S(1)} %copy-done), kind=kOutput, calls=%fused_computation.3 | convolution fusion | flops 3221225472 | bytes 5242880 | tf_op jit(solution)/shard_map/dot_general | solution.py:24
  213.8 238.5 %while.10 = (s32[]{:T(128)}, f32[512,1024]{0,1:T(8,128)}, f32[512,1024]{0,1:T(8,128)S(1)}, f32[512,512]{1,0:T(8,128)S(1)}, s32[]{:T(128)}) while((s32[]{:T(128)}, f32[512,1024]{0,1:T(8,128)}, f32[512,1024]{0,1:T(8,128)S(1)}, f32[512,512]{1,0:T(8,128)S(1)}, s32[]{:T(128)}) %tuple.22), condition=%wide.region_1.0_spmd, body=%wide.region_0.0_spmd.sunk | while | flops 3221749760 | bytes 15728741 | solution.py:44
  214.1 1.9 collective-permute-start
  216.0 25.7 %collective-permute-done = f32[512,1024]{0,1:T(8,128)} collective-permute-done((f32[512,1024]{0,1:T(8,128)}, f32[512,1024]{0,1:T(8,128)}, u32[]{:S(2)}, u32[]{:S(2)}) %collective-permute-start) | collective-permute-done | bytes 2097184 | tf_op jit(solution)/shard_map/while/body/eval_jaxpr/ppermute | solution.py:20
  241.8 6.4 %fusion.25 = f32[512,1024]{0,1:T(8,128)} fusion(f32[512,512]{1,0:T(8,128)S(1)} %get-tuple-element.74, f32[512,1024]{0,1:T(8,128)} %collective-permute-done, f32[512,1024]{0,1:T(8,128)S(1)} %get-tuple-element.73), kind=kOutput, calls=%fused_computation.2.clone.1 | convolution fusion | flops 3221749760 | bytes 7340032 | tf_op jit(solution)/shard_map/while/body/eval_jaxpr/dot_general | solution.py:24
  250.0 25.7 %collective-permute-done = f32[512,1024]{0,1:T(8,128)} collective-permute-done((f32[512,1024]{0,1:T(8,128)}, f32[512,1024]{0,1:T(8,128)}, u32[]{:S(2)}, u32[]{:S(2)}) %collective-permute-start) | collective-permute-done | bytes 2097184 | tf_op jit(solution)/shard_map/while/body/eval_jaxpr/ppermute | solution.py:20
  275.8 6.4 %fusion.25 = f32[512,1024]{0,1:T(8,128)} fusion(f32[512,512]{1,0:T(8,128)S(1)} %get-tuple-element.74, f32[512,1024]{0,1:T(8,128)} %collective-permute-done, f32[512,1024]{0,1:T(8,128)S(1)} %get-tuple-element.73), kind=kOutput, calls=%fused_computation.2.clone.1 | convolution fusion | flops 3221749760 | bytes 7340032 | tf_op jit(solution)/shard_map/while/body/eval_jaxpr/dot_general | solution.py:24
  284.1 25.7 %collective-permute-done = f32[512,1024]{0,1:T(8,128)} collective-permute-done((f32[512,1024]{0,1:T(8,128)}, f32[512,1024]{0,1:T(8,128)}, u32[]{:S(2)}, u32[]{:S(2)}) %collective-permute-start) | collective-permute-done | bytes 2097184 | tf_op jit(solution)/shard_map/while/body/eval_jaxpr/ppermute | solution.py:20
  309.8 6.4 %fusion.25 = f32[512,1024]{0,1:T(8,128)} fusion(f32[512,512]{1,0:T(8,128)S(1)} %get-tuple-element.74, f32[512,1024]{0,1:T(8,128)} %collective-permute-done, f32[512,1024]{0,1:T(8,128)S(1)} %get-tuple-element.73), kind=kOutput, calls=%fused_computation.2.clone.1 | convolution fusion | flops 3221749760 | bytes 7340032 | tf_op jit(solution)/shard_map/while/body/eval_jaxpr/dot_general | solution.py:24
  318.1 25.7 %collective-permute-done = f32[512,1024]{0,1:T(8,128)} collective-permute-done((f32[512,1024]{0,1:T(8,128)}, f32[512,1024]{0,1:T(8,128)}, u32[]{:S(2)}, u32[]{:S(2)}) %collective-permute-start) | collective-permute-done | bytes 2097184 | tf_op jit(solution)/shard_map/while/body/eval_jaxpr/ppermute | solution.py:20
  343.8 6.4 %fusion.25 = f32[512,1024]{0,1:T(8,128)} fusion(f32[512,512]{1,0:T(8,128)S(1)} %get-tuple-element.74, f32[512,1024]{0,1:T(8,128)} %collective-permute-done, f32[512,1024]{0,1:T(8,128)S(1)} %get-tuple-element.73), kind=kOutput, calls=%fused_computation.2.clone.1 | convolution fusion | flops 3221749760 | bytes 7340032 | tf_op jit(solution)/shard_map/while/body/eval_jaxpr/dot_general | solution.py:24
  352.1 25.7 %collective-permute-done = f32[512,1024]{0,1:T(8,128)} collective-permute-done((f32[512,1024]{0,1:T(8,128)}, f32[512,1024]{0,1:T(8,128)}, u32[]{:S(2)}, u32[]{:S(2)}) %collective-permute-start) | collective-permute-done | bytes 2097184 | tf_op jit(solution)/shard_map/while/body/eval_jaxpr/ppermute | solution.py:20
  377.9 6.4 %fusion.25 = f32[512,1024]{0,1:T(8,128)} fusion(f32[512,512]{1,0:T(8,128)S(1)} %get-tuple-element.74, f32[512,1024]{0,1:T(8,128)} %collective-permute-done, f32[512,1024]{0,1:T(8,128)S(1)} %get-tuple-element.73), kind=kOutput, calls=%fused_computation.2.clone.1 | convolution fusion | flops 3221749760 | bytes 7340032 | tf_op jit(solution)/shard_map/while/body/eval_jaxpr/dot_general | solution.py:24
  386.2 25.7 %collective-permute-done = f32[512,1024]{0,1:T(8,128)} collective-permute-done((f32[512,1024]{0,1:T(8,128)}, f32[512,1024]{0,1:T(8,128)}, u32[]{:S(2)}, u32[]{:S(2)}) %collective-permute-start) | collective-permute-done | bytes 2097184 | tf_op jit(solution)/shard_map/while/body/eval_jaxpr/ppermute | solution.py:20
  411.9 6.4 %fusion.25 = f32[512,1024]{0,1:T(8,128)} fusion(f32[512,512]{1,0:T(8,128)S(1)} %get-tuple-element.74, f32[512,1024]{0,1:T(8,128)} %collective-permute-done, f32[512,1024]{0,1:T(8,128)S(1)} %get-tuple-element.73), kind=kOutput, calls=%fused_computation.2.clone.1 | convolution fusion | flops 3221749760 | bytes 7340032 | tf_op jit(solution)/shard_map/while/body/eval_jaxpr/dot_general | solution.py:24
  420.2 25.7 %collective-permute-done = f32[512,1024]{0,1:T(8,128)} collective-permute-done((f32[512,1024]{0,1:T(8,128)}, f32[512,1024]{0,1:T(8,128)}, u32[]{:S(2)}, u32[]{:S(2)}) %collective-permute-start) | collective-permute-done | bytes 2097184 | tf_op jit(solution)/shard_map/while/body/eval_jaxpr/ppermute | solution.py:20
  445.9 6.4 %fusion.25 = f32[512,1024]{0,1:T(8,128)} fusion(f32[512,512]{1,0:T(8,128)S(1)} %get-tuple-element.74, f32[512,1024]{0,1:T(8,128)} %collective-permute-done, f32[512,1024]{0,1:T(8,128)S(1)} %get-tuple-element.73), kind=kOutput, calls=%fused_computation.2.clone.1 | convolution fusion | flops 3221749760 | bytes 7340032 | tf_op jit(solution)/shard_map/while/body/eval_jaxpr/dot_general | solution.py:24
  452.3 2.9 copy.4
  (12 shorter events, 14.6 us)
Async XLA Ops:
  0.0 47.6 %collective-permute-start.1 = (f32[512,1024]{1,0:T(8,128)}, f32[512,1024]{1,0:T(8,128)S(1)}, u32[]{:S(2)}, u32[]{:S(2)}) collective-permute-start(f32[512,1024]{1,0:T(8,128)} %bitcast.64), channel_id=1, source_target_pairs={{0,1},{1,0},{2,3},{3,2},{4,5},{5,4},{6,7},{7,6},{8,9},{9,8},{10,11... | collective-permute-start | bytes 6291464 | tf_op jit(solution)/shard_map/ppermute | solution.py:14
  1.5 54.2 %copy-start.1 = (f32[4,1,1,512,1024]{4,3,2,1,0:T(8,128)S(1)}, f32[4,1,1,512,1024]{4,3,2,1,0:T(8,128)}, u32[]{:S(2)}) copy-start(f32[4,1,1,512,1024]{4,3,2,1,0:T(8,128)} %param.6) | copy-start | bytes 25165828
  52.4 48.3 %collective-permute-start.2 = (f32[512,1024]{1,0:T(8,128)S(1)}, f32[512,1024]{1,0:T(8,128)S(1)}, u32[]{:S(2)}, u32[]{:S(2)}) collective-permute-start(f32[512,1024]{1,0:T(8,128)S(1)} %convolution_add_fusion.3), channel_id=1, source_target_pairs={{0,2},{2,0},{1,3},{3,1},{4,6},{6,4},{5,7},{7,5},{8,10},{10,8},{9,1... | collective-permute-start | bytes 6291464 | tf_op jit(solution)/shard_map/ppermute | solution.py:14
  107.7 45.7 %collective-permute-start.3 = (f32[512,1024]{0,1:T(8,128)S(1)}, f32[512,1024]{0,1:T(8,128)S(1)}, u32[]{:S(2)}, u32[]{:S(2)}) collective-permute-start(f32[512,1024]{0,1:T(8,128)S(1)} %bitcast.63), channel_id=1, source_target_pairs={{0,4},{4,0},{1,5},{5,1},{2,6},{6,2},{3,7},{7,3},{8,12},{12,8},{9,1... | collective-permute-start | bytes 6291464 | tf_op jit(solution)/shard_map/ppermute | solution.py:14
  157.0 46.6 %collective-permute-start.4 = (f32[512,1024]{0,1:T(8,128)S(1)}, f32[512,1024]{0,1:T(8,128)}, u32[]{:S(2)}, u32[]{:S(2)}) collective-permute-start(f32[512,1024]{0,1:T(8,128)S(1)} %bitcast.62), channel_id=1, source_target_pairs={{0,8},{8,0},{1,9},{9,1},{2,10},{10,2},{3,11},{11,3},{4,12},{12,4},... | collective-permute-start | bytes 6291464 | tf_op jit(solution)/shard_map/ppermute | solution.py:14
  165.2 43.8 %copy-start = (f32[1,1,512,512]{3,2,1,0:T(8,128)S(1)}, f32[1,1,512,512]{3,2,1,0:T(8,128)}, u32[]{:S(2)}) copy-start(f32[1,1,512,512]{3,2,1,0:T(8,128)} %param.7) | copy-start | bytes 3145732
  214.1 27.7 %collective-permute-start = (f32[512,1024]{0,1:T(8,128)}, f32[512,1024]{0,1:T(8,128)}, u32[]{:S(2)}, u32[]{:S(2)}) collective-permute-start(f32[512,1024]{0,1:T(8,128)} %get-tuple-element.67), channel_id=1, source_target_pairs={{0,16},{16,32},{32,48},{48,64},{64,80},{80,96},{96,112},{1,17},{17... | collective-permute-start | bytes 6291464 | tf_op jit(solution)/shard_map/while/body/eval_jaxpr/ppermute | solution.py:20
  248.1 27.7 %collective-permute-start = (f32[512,1024]{0,1:T(8,128)}, f32[512,1024]{0,1:T(8,128)}, u32[]{:S(2)}, u32[]{:S(2)}) collective-permute-start(f32[512,1024]{0,1:T(8,128)} %get-tuple-element.67), channel_id=1, source_target_pairs={{0,16},{16,32},{32,48},{48,64},{64,80},{80,96},{96,112},{1,17},{17... | collective-permute-start | bytes 6291464 | tf_op jit(solution)/shard_map/while/body/eval_jaxpr/ppermute | solution.py:20
  282.2 27.7 %collective-permute-start = (f32[512,1024]{0,1:T(8,128)}, f32[512,1024]{0,1:T(8,128)}, u32[]{:S(2)}, u32[]{:S(2)}) collective-permute-start(f32[512,1024]{0,1:T(8,128)} %get-tuple-element.67), channel_id=1, source_target_pairs={{0,16},{16,32},{32,48},{48,64},{64,80},{80,96},{96,112},{1,17},{17... | collective-permute-start | bytes 6291464 | tf_op jit(solution)/shard_map/while/body/eval_jaxpr/ppermute | solution.py:20
  316.2 27.7 %collective-permute-start = (f32[512,1024]{0,1:T(8,128)}, f32[512,1024]{0,1:T(8,128)}, u32[]{:S(2)}, u32[]{:S(2)}) collective-permute-start(f32[512,1024]{0,1:T(8,128)} %get-tuple-element.67), channel_id=1, source_target_pairs={{0,16},{16,32},{32,48},{48,64},{64,80},{80,96},{96,112},{1,17},{17... | collective-permute-start | bytes 6291464 | tf_op jit(solution)/shard_map/while/body/eval_jaxpr/ppermute | solution.py:20
  350.2 27.7 %collective-permute-start = (f32[512,1024]{0,1:T(8,128)}, f32[512,1024]{0,1:T(8,128)}, u32[]{:S(2)}, u32[]{:S(2)}) collective-permute-start(f32[512,1024]{0,1:T(8,128)} %get-tuple-element.67), channel_id=1, source_target_pairs={{0,16},{16,32},{32,48},{48,64},{64,80},{80,96},{96,112},{1,17},{17... | collective-permute-start | bytes 6291464 | tf_op jit(solution)/shard_map/while/body/eval_jaxpr/ppermute | solution.py:20
  384.2 27.7 %collective-permute-start = (f32[512,1024]{0,1:T(8,128)}, f32[512,1024]{0,1:T(8,128)}, u32[]{:S(2)}, u32[]{:S(2)}) collective-permute-start(f32[512,1024]{0,1:T(8,128)} %get-tuple-element.67), channel_id=1, source_target_pairs={{0,16},{16,32},{32,48},{48,64},{64,80},{80,96},{96,112},{1,17},{17... | collective-permute-start | bytes 6291464 | tf_op jit(solution)/shard_map/while/body/eval_jaxpr/ppermute | solution.py:20
  418.3 27.7 %collective-permute-start = (f32[512,1024]{0,1:T(8,128)}, f32[512,1024]{0,1:T(8,128)}, u32[]{:S(2)}, u32[]{:S(2)}) collective-permute-start(f32[512,1024]{0,1:T(8,128)} %get-tuple-element.67), channel_id=1, source_target_pairs={{0,16},{16,32},{32,48},{48,64},{64,80},{80,96},{96,112},{1,17},{17... | collective-permute-start | bytes 6291464 | tf_op jit(solution)/shard_map/while/body/eval_jaxpr/ppermute | solution.py:20
where the time goes:
time: 462 us; the launch traced here: 456 us
  waiting for transfers between devices  338 us (73%)
  matrix products  90.9 us (20%)
  starting transfers between devices  23.3 us (5%)
    ppermute x7, waiting for transfers between devices, shifted(): return lax.ppermute(value, axis, pairs)  180 us
    ppermute x4, waiting for transfers between devices, partner_2(): return lax.ppermute(block, axis, route)  157 us
    dot_general x16, matrix products, product(): jnp.dot(left, right, preferred_element_type=jnp.float32, precision=lax.Pr...  90.9 us
    ppermute x7, starting transfers between devices, shifted(): return lax.ppermute(value, axis, pairs)  13.4 us
    ppermute x4, starting transfers between devices, partner_2(): return lax.ppermute(block, axis, route)  9.95 us
  transfers between devices with their start and end apart: 11, of which 11 were waited for; matrix products, arithmetic and copies ran while one was open for 5% of the time, Pallas kernels for 0%

commit v1 on v0

v1 whole, which is shorter than its diff:
```python
import functools

import jax
import jax.numpy as jnp
from jax import lax
from jax.experimental import pallas as pl
from jax.experimental.pallas import tpu as pltpu
from jax.sharding import PartitionSpec as P

MESH = pl.DeviceIdType.MESH
F32 = jnp.float32
BF16 = jnp.bfloat16
F = 512
COLS = 1024
LEVELS = 4
CHIPS = 4
BLOCK = 128
C = 64
N = COLS // C
AHEAD = 2


def halves(value):
    high = value.astype(BF16)
    return high, (value - high.astype(F32)).astype(BF16)


def product(left, high, low):
    rows = left.shape[0]
    left_high, left_low = halves(left)
    both = jnp.dot(
        jnp.concatenate([left_high, left_low], axis=0), high, preferred_element_type=F32
    )
    return both[:rows] + both[rows:] + jnp.dot(left_high, low, preferred_element_type=F32)


def kernel(
    src, merge, sweep, out,
    src_stage, merge_stage, sweep_stage, sweep_turned, even_turned,
    state, arrived, from_even, carried, result,
    merge_high, merge_low, sweep_high, sweep_low,
    load_sem, send_sem, recv_sem, even_send, even_recv, op_send, op_recv,
    carry_send, carry_recv,
):
    slab = lax.axis_index("slab")
    leaf = lax.axis_index("leaf")
    z, core = lax.div(slab, 2), lax.rem(slab, 2)
    y, x = lax.div(leaf, 4), lax.rem(leaf, 4)
    partner = (
        (slab, y * 4 + x + 1 - 2 * lax.rem(x, 2)),
        (slab, y * 4 + lax.rem(x + 2, 4)),
        (slab, (y + 1 - 2 * lax.rem(y, 2)) * 4 + x),
        (slab, lax.rem(y + 2, 4) * 4 + x),
    )
    sibling = (slab + 1 - 2 * core, leaf)

    def load_source(block):
        return pltpu.make_async_copy(
            src.at[0, 0, :, pl.ds(pl.multiple_of(block * BLOCK, BLOCK), BLOCK)],
            src_stage.at[block], load_sem.at[block],
        )

    def load_merge(level):
        return pltpu.make_async_copy(
            merge.at[level, 0, 0], merge_stage.at[level], load_sem.at[COLS // BLOCK + level]
        )

    load_sweep = pltpu.make_async_copy(
        sweep.at[0, 0], sweep_stage, load_sem.at[COLS // BLOCK + LEVELS]
    )

    load_source(0).start()
    load_merge(0).start()
    for block in range(1, COLS // BLOCK):
        load_source(block).start()
    for level in range(1, LEVELS):
        load_merge(level).start()
    load_sweep.start()

    barrier = pltpu.get_barrier_semaphore()
    for device in partner + (sibling,):
        pl.semaphore_signal(barrier, inc=1, device_id=device, device_id_type=MESH)

    @pl.when(z > 0)
    def _():
        pl.semaphore_signal(
            barrier, inc=1, device_id=(2 * (z - 1) + 1, leaf), device_id_type=MESH
        )

    below = lax.div(z + 1, CHIPS)
    pl.semaphore_wait(barrier, 5 + 2 * core * (1 - below))

    def rows(chunk):
        return pl.ds(pl.multiple_of(chunk * C, C), C)

    def exchange(level, chunk):
        return pltpu.make_async_remote_copy(
            src_ref=state.at[level, rows(chunk)],
            dst_ref=arrived.at[level, rows(chunk)],
            send_sem=send_sem.at[level, chunk],
            recv_sem=recv_sem.at[level, chunk],
            device_id=partner[level],
            device_id_type=MESH,
        )

    def to_odd(chunk):
        return pltpu.make_async_remote_copy(
            src_ref=state.at[LEVELS, rows(chunk)],
            dst_ref=from_even.at[rows(chunk)],
            send_sem=even_send.at[chunk],
            recv_sem=even_recv.at[chunk],
            device_id=sibling,
            device_id_type=MESH,
        )

    operator_copy = pltpu.make_async_remote_copy(
        src_ref=sweep_turned,
        dst_ref=even_turned,
        send_sem=op_send,
        recv_sem=op_recv,
        device_id=sibling,
        device_id_type=MESH,
    )

    def carry(chunk, target):
        return pltpu.make_async_remote_copy(
            src_ref=result.at[rows(chunk)],
            dst_ref=carried.at[rows(chunk)],
            send_sem=carry_send.at[target, chunk],
            recv_sem=carry_recv.at[chunk],
            device_id=(2 * (z + 1) + target, leaf),
            device_id_type=MESH,
        )

    def turn_source(block):
        load_source(block).wait()
        state[0, pl.ds(pl.multiple_of(block * BLOCK, BLOCK), BLOCK)] = src_stage[block].T

    def prepare_merge(level):
        load_merge(level).wait()

        def turn(step, _):
            at = pl.ds(pl.multiple_of(step * BLOCK, BLOCK), BLOCK)
            high, low = halves(merge_stage[level, :, at].T)
            merge_high[level, at] = high
            merge_low[level, at] = low
            return 0

        lax.fori_loop(0, 2 * F // BLOCK, turn, 0)

    def prepare_sweep():
        load_sweep.wait()

        def turn(step, _):
            at = pl.ds(pl.multiple_of(step * BLOCK, BLOCK), BLOCK)
            turned = sweep_stage[:, at].T
            high, low = halves(turned)
            sweep_turned[at] = turned
            sweep_high[at] = high
            sweep_low[at] = low
            return 0

        lax.fori_loop(0, F // BLOCK, turn, 0)

        @pl.when(core == 0)
        def _():
            operator_copy.start()

    def compose_sweep():
        @pl.when(core == 1)
        def _():
            operator_copy.wait_recv()

            def compose(step, _):
                at = pl.ds(pl.multiple_of(step * BLOCK, BLOCK), BLOCK)
                to = pl.ds(pl.multiple_of(F + step * BLOCK, BLOCK), BLOCK)
                high, low = halves(product(even_turned[at], sweep_high[:F], sweep_low[:F]))
                sweep_high[to] = high
                sweep_low[to] = low
                return 0

            lax.fori_loop(0, F // BLOCK, compose, 0)

    turn_source(0)
    for chunk in range(AHEAD):
        exchange(0, chunk).start()
    prepare_merge(0)
    per_block = BLOCK // C

    def step(k, _):
        for level in range(1, LEVELS):
            pl.when(k == level - 1)(functools.partial(prepare_merge, level))
        pl.when(k == LEVELS - 2)(prepare_sweep)
        pl.when(k == LEVELS - 1)(compose_sweep)

        ahead = k + AHEAD

        @pl.when((ahead < N) & (lax.rem(ahead, per_block) == 0))
        def _():
            turn_source(lax.div(ahead, per_block))

        for level in range(LEVELS):
            chunk = k - level

            @pl.when((chunk >= 0) & (chunk < N))
            def _():
                exchange(level, chunk).wait_recv()
                left = jnp.concatenate(
                    [state[level, rows(chunk)], arrived[level, rows(chunk)]], axis=1
                )
                state[level + 1, rows(chunk)] = product(
                    left, merge_high[level], merge_low[level]
                )
                if level < LEVELS - 1:
                    exchange(level + 1, chunk).start()
                else:
                    @pl.when(core == 0)
                    def _():
                        to_odd(chunk).start()

            if level == 0:
                @pl.when(ahead < N)
                def _():
                    exchange(0, ahead).start()

        chunk = k - LEVELS - z
        inside = (chunk >= 0) & (chunk < N)

        @pl.when(inside & (z > 0))
        def _():
            carry(chunk, 0).wait_recv()

        @pl.when(inside & (z == 0))
        def _():
            carried[rows(chunk)] = jnp.zeros((C, F), F32)

        @pl.when(inside & (core == 0))
        def _():
            left = state[LEVELS, rows(chunk)] + carried[rows(chunk)]
            result[rows(chunk)] = product(left, sweep_high[:F], sweep_low[:F])

        @pl.when(inside & (core == 1))
        def _():
            to_odd(chunk).wait_recv()
            left = jnp.concatenate(
                [state[LEVELS, rows(chunk)], from_even[rows(chunk)] + carried[rows(chunk)]],
                axis=1,
            )
            result[rows(chunk)] = product(left, sweep_high[...], sweep_low[...])

            @pl.when(z < CHIPS - 1)
            def _():
                carry(chunk, 1).start()
                carry(chunk, 0).start()

        @pl.when(inside & (lax.rem(chunk, per_block) == per_block - 1))
        def _():
            block = lax.div(chunk, per_block)
            at = pl.ds(pl.multiple_of(block * BLOCK, BLOCK), BLOCK)
            out[:, at] = result[at].T

        return 0

    lax.fori_loop(0, N + LEVELS + CHIPS - 1, step, 0)

    def finish(chunk, _):
        for level in range(LEVELS):
            exchange(level, chunk).wait_send()

        @pl.when(core == 0)
        def _():
            to_odd(chunk).wait_send()

        @pl.when((core == 1) & (z < CHIPS - 1))
        def _():
            carry(chunk, 0).wait_send()
            carry(chunk, 1).wait_send()

        return 0

    lax.fori_loop(0, N, finish, 0)

    @pl.when(core == 0)
    def _():
        operator_copy.wait_send()


def per_device(sources, merge_ops, sweep_ops):
    anywhere = pl.BlockSpec(memory_space=pl.ANY)
    dma = pltpu.SemaphoreType.DMA
    interface = pl.pallas_call(
        kernel,
        out_shape=jax.ShapeDtypeStruct((F, COLS), F32),
        in_specs=[anywhere] * 3,
        out_specs=pl.BlockSpec(memory_space=pltpu.VMEM),
        scratch_shapes=[
            pltpu.VMEM((COLS // BLOCK, F, BLOCK), F32),
            pltpu.VMEM((LEVELS, F, 2 * F), F32),
            pltpu.VMEM((F, F), F32),
            pltpu.VMEM((F, F), F32),
            pltpu.VMEM((F, F), F32),
            pltpu.VMEM((LEVELS + 1, COLS, F), F32),
            pltpu.VMEM((LEVELS, COLS, F), F32),
            pltpu.VMEM((COLS, F), F32),
            pltpu.VMEM((COLS, F), F32),
            pltpu.VMEM((COLS, F), F32),
            pltpu.VMEM((LEVELS, 2 * F, F), BF16),
            pltpu.VMEM((LEVELS, 2 * F, F), BF16),
            pltpu.VMEM((2 * F, F), BF16),
            pltpu.VMEM((2 * F, F), BF16),
            dma((COLS // BLOCK + LEVELS + 1,)),
            dma((LEVELS, N)),
            dma((LEVELS, N)),
            dma((N,)),
            dma((N,)),
            dma,
            dma,
            dma((2, N)),
            dma((N,)),
        ],
        compiler_params=pltpu.CompilerParams(
            collective_id=0, has_side_effects=True, vmem_limit_bytes=60 << 20
        ),
        cost_estimate=pl.CostEstimate(
            flops=3 * 10 * F * F * COLS, bytes_accessed=15 << 20, transcendentals=0
        ),
        name="solve",
    )(sources, merge_ops, sweep_ops)
    return interface[None, None]


def solution(mesh):
    in_specs = (
        P("slab", "leaf", None, None),
        P(None, "slab", "leaf", None, None),
        P("slab", "leaf", None, None),
    )
    out_specs = P("slab", "leaf", None, None)
    return jax.shard_map(
        per_device, mesh=mesh, in_specs=in_specs, out_specs=out_specs, check_vma=False
    )
```

time: 462 us -> 131 us (0.28); the launches traced: 456 us -> 131 us
  waiting for transfers between devices: 338 us -> 0 us
  Pallas kernels: 0 us -> 128 us
  matrix products: 90.9 us -> 0 us
  starting transfers between devices: 23.3 us -> 0 us
    ppermute x11 -> x0, waiting for transfers between devices: 338 us -> none  [the longest x7 180 us: shifted(): return lax.ppermute(value, axis, pairs)]
    pallas_call x0 -> x1, Pallas kernels: none -> 128 us  [per_device(): pl.pallas_call(kernel, out_shape=jax.ShapeDtypeStruct((F, COLS), F32), in...]
    dot_general x16 -> x0, matrix products: 90.9 us -> none  [product(): jnp.dot(left, right, preferred_element_type=jnp.float32, precision=lax.Pr...]
    ppermute x11 -> x0, starting transfers between devices: 23.3 us -> none  [the longest x7 13.4 us: shifted(): return lax.ppermute(value, axis, pairs)]
  transfers between devices with their start and end apart: 11 -> 0, of which waited for: 11 -> 0; matrix products, arithmetic and copies ran while one was open for 5% -> 0% of each run, Pallas kernels for 0% -> 0%
where the time goes in v1:
time: 131 us
  Pallas kernels  128 us (98%)
  local copies, waits for them, and re-layouts  3.16 us (2%)
    pallas_call x1, Pallas kernels, per_device(): pl.pallas_call(kernel, out_shape=jax.ShapeDtypeStruct((F, COLS), F32), in...  128 us
    unnamed x1, local copies, waits for them, and re-layouts  3.16 us

profile of v1, /device:TPU:96, one launch (start us, length us, event | category | flops | bytes accessed | tf_op | source)
XLA Modules:
  0.0 131.1 jit_solution(11703544540920192045)
XLA Ops:
  0.0 128.0 %solve.1 = f32[512,1024]{1,0:T(8,128)} custom-call(f32[1,1,512,1024]{3,2,1,0:T(8,128)} %src.1, f32[4,1,1,512,1024]{4,3,2,1,0:T(8,128)} %merge.1, f32[1,1,512,512]{3,2,1,0:T(8,128)} %sweep.1), custom_call_target="tpu_custom_call" | custom-call | flops 8053063680 | bytes 15728640 | tf_op jit(solution)/shard_map/solve/pallas_call | solution.py:291
  128.0 3.2 %copy.5 = f32[1,1,512,1024]{3,2,1,0:T(8,128)} copy(f32[1,1,512,1024]{3,2,1,0:T(8,128)} %bitcast.1) | data formatting | bytes 4194304

commit v2 on v1

v2 whole, which is shorter than its diff:
```python
import functools

import jax
import jax.numpy as jnp
from jax import lax
from jax.experimental import pallas as pl
from jax.experimental.pallas import tpu as pltpu
from jax.sharding import PartitionSpec as P

MESH = pl.DeviceIdType.MESH
F32 = jnp.float32
BF16 = jnp.bfloat16
F = 512
COLS = 1024
LEVELS = 4
CHIPS = 4
BLOCK = 128
C = 64
N = COLS // C
AHEAD = 2
PIECES = 2
PIECE = C // PIECES
PARTS = 4


def halves(value):
    high = value.astype(BF16)
    return high, (value - high.astype(F32)).astype(BF16)


def product(left, high, low):
    rows = left.shape[0]
    left_high, left_low = halves(left)
    both = jnp.dot(
        jnp.concatenate([left_high, left_low], axis=0), high, preferred_element_type=F32
    )
    return both[:rows] + both[rows:] + jnp.dot(left_high, low, preferred_element_type=F32)


def kernel(
    src, merge, sweep, out,
    src_stage, merge_stage, sweep_stage, sweep_turned, even_turned,
    state, arrived, from_even, carried, result, out_stage,
    merge_high, merge_low, sweep_high, sweep_low,
    load_sem, send_sem, recv_sem, even_send, even_recv, op_send, op_recv,
    carry_send, carry_recv, pass_send, pass_recv, store_sem,
):
    slab = lax.axis_index("slab")
    leaf = lax.axis_index("leaf")
    z, core = lax.div(slab, 2), lax.rem(slab, 2)
    y, x = lax.div(leaf, 4), lax.rem(leaf, 4)
    partner = (
        (slab, y * 4 + x + 1 - 2 * lax.rem(x, 2)),
        (slab, y * 4 + lax.rem(x + 2, 4)),
        (slab, (y + 1 - 2 * lax.rem(y, 2)) * 4 + x),
        (slab, lax.rem(y + 2, 4) * 4 + x),
    )
    sibling = (slab + 1 - 2 * core, leaf)
    blocks = COLS // BLOCK
    per_block = BLOCK // C

    def at_block(block):
        return pl.ds(pl.multiple_of(block * BLOCK, BLOCK), BLOCK)

    def load_source(block):
        return pltpu.make_async_copy(
            src.at[0, 0, :, at_block(block)], src_stage.at[block], load_sem.at[block]
        )

    def load_merge(level):
        return pltpu.make_async_copy(
            merge.at[level, 0, 0], merge_stage.at[level], load_sem.at[blocks + level]
        )

    load_sweep = pltpu.make_async_copy(
        sweep.at[0, 0], sweep_stage, load_sem.at[blocks + LEVELS]
    )

    load_source(0).start()
    load_merge(0).start()
    for block in range(1, blocks):
        load_source(block).start()
    for level in range(1, LEVELS):
        load_merge(level).start()
    load_sweep.start()

    barrier = pltpu.get_barrier_semaphore()
    for device in partner + (sibling,):
        pl.semaphore_signal(barrier, inc=1, device_id=device, device_id_type=MESH)

    @pl.when((z > 0) & (core == 1))
    def _():
        pl.semaphore_signal(barrier, inc=1, device_id=(slab - 2, leaf), device_id_type=MESH)

    last = lax.div(z + 1, CHIPS)
    pl.semaphore_wait(barrier, 5 + core * (1 - last))

    def rows(chunk):
        return pl.ds(pl.multiple_of(chunk * C, C), C)

    def piece_rows(chunk, piece):
        return pl.ds(pl.multiple_of(chunk * C + piece * PIECE, PIECE), PIECE)

    def exchange(level, chunk):
        return pltpu.make_async_remote_copy(
            src_ref=state.at[level, rows(chunk)],
            dst_ref=arrived.at[level, rows(chunk)],
            send_sem=send_sem.at[level, chunk],
            recv_sem=recv_sem.at[level, chunk],
            device_id=partner[level],
            device_id_type=MESH,
        )

    def to_odd(chunk):
        return pltpu.make_async_remote_copy(
            src_ref=state.at[LEVELS, rows(chunk)],
            dst_ref=from_even.at[rows(chunk)],
            send_sem=even_send.at[chunk],
            recv_sem=even_recv.at[chunk],
            device_id=sibling,
            device_id_type=MESH,
        )

    operator_copy = pltpu.make_async_remote_copy(
        src_ref=sweep_turned,
        dst_ref=even_turned,
        send_sem=op_send,
        recv_sem=op_recv,
        device_id=sibling,
        device_id_type=MESH,
    )

    def carry(chunk, piece):
        return pltpu.make_async_remote_copy(
            src_ref=result.at[piece_rows(chunk, piece)],
            dst_ref=carried.at[piece_rows(chunk, piece)],
            send_sem=carry_send.at[piece, chunk],
            recv_sem=carry_recv.at[piece, chunk],
            device_id=(slab + 2, leaf),
            device_id_type=MESH,
        )

    def pass_on(chunk, piece):
        return pltpu.make_async_remote_copy(
            src_ref=carried.at[piece_rows(chunk, piece)],
            dst_ref=carried.at[piece_rows(chunk, piece)],
            send_sem=pass_send.at[piece, chunk],
            recv_sem=pass_recv.at[piece, chunk],
            device_id=sibling,
            device_id_type=MESH,
        )

    def store(block):
        return pltpu.make_async_copy(
            out_stage.at[block], out.at[:, at_block(block)], store_sem.at[block]
        )

    def turn_source(block):
        load_source(block).wait()
        state[0, at_block(block)] = src_stage[block].T

    def prepare_merge(level):
        load_merge(level).wait()

        def turn(step, _):
            at = at_block(step)
            high, low = halves(merge_stage[level, :, at].T)
            merge_high[level, at] = high
            merge_low[level, at] = low
            return 0

        lax.fori_loop(0, 2 * F // BLOCK, turn, 0)

    def prepare_sweep():
        load_sweep.wait()

        def turn(step, _):
            at = at_block(step)
            to = at_block(F // BLOCK + step)
            turned = sweep_stage[:, at].T
            high, low = halves(turned)
            sweep_turned[at] = turned
            sweep_high[at] = high
            sweep_low[at] = low
            sweep_high[to] = high
            sweep_low[to] = low
            return 0

        lax.fori_loop(0, F // BLOCK, turn, 0)

        @pl.when(core == 0)
        def _():
            operator_copy.start()

    def compose_sweep():
        @pl.when(core == 1)
        def _():
            operator_copy.wait_recv()

            def compose(step, _):
                at = at_block(step)
                to = at_block(F // BLOCK + step)
                high, low = halves(product(even_turned[at], sweep_high[:F], sweep_low[:F]))
                sweep_high[to] = high
                sweep_low[to] = low
                return 0

            lax.fori_loop(0, F // BLOCK, compose, 0)

    for block in range(-(-AHEAD * C // BLOCK)):
        turn_source(block)
    for chunk in range(AHEAD):
        exchange(0, chunk).start()
    prepare_merge(0)

    def step(k, _):
        for level in range(1, LEVELS):
            pl.when(k == level - 1)(functools.partial(prepare_merge, level))
        pl.when(k == LEVELS - 2)(prepare_sweep)
        pl.when(k == LEVELS - 1)(compose_sweep)

        ahead = k + AHEAD

        @pl.when((ahead < N) & (lax.rem(ahead, per_block) == 0))
        def _():
            turn_source(lax.div(ahead, per_block))

        for level in range(LEVELS):
            chunk = k - level

            @pl.when((chunk >= 0) & (chunk < N))
            def _():
                own = product(
                    state[level, rows(chunk)], merge_high[level, :F], merge_low[level, :F]
                )
                exchange(level, chunk).wait_recv()
                state[level + 1, rows(chunk)] = own + product(
                    arrived[level, rows(chunk)], merge_high[level, F:], merge_low[level, F:]
                )
                if level < LEVELS - 1:
                    exchange(level + 1, chunk).start()
                else:
                    @pl.when(core == 0)
                    def _():
                        to_odd(chunk).start()

                if level > 0:
                    exchange(level - 1, chunk).wait_send()

            if level == 0:
                @pl.when(ahead < N)
                def _():
                    exchange(0, ahead).start()

        chunk = k - LEVELS

        @pl.when((chunk >= 0) & (chunk < N))
        def _():
            result[rows(chunk)] = product(
                state[LEVELS, rows(chunk)], sweep_high[:F], sweep_low[:F]
            )

            @pl.when(core == 1)
            def _():
                to_odd(chunk).wait_recv()
                result[rows(chunk)] += product(
                    from_even[rows(chunk)], sweep_high[F:], sweep_low[F:]
                )

                @pl.when(z == 0)
                def _():
                    for piece in range(PIECES):
                        carry(chunk, piece).start()

            exchange(LEVELS - 1, chunk).wait_send()

            @pl.when(core == 0)
            def _():
                to_odd(chunk).wait_send()

        chunk = k - LEVELS - z
        inside = (chunk >= 0) & (chunk < N)

        @pl.when(inside & (z > 0))
        def _():
            for piece in range(PIECES):
                @pl.when(core == 1)
                def _():
                    carry(chunk, piece).wait_recv()
                    pass_on(chunk, piece).start()

                @pl.when(core == 0)
                def _():
                    pass_on(chunk, piece).wait_recv()

                at = piece_rows(chunk, piece)
                result[at] += product(carried[at], sweep_high[F:], sweep_low[F:])

                @pl.when((core == 1) & (z < CHIPS - 1))
                def _():
                    carry(chunk, piece).start()

        @pl.when(inside & (lax.rem(chunk, per_block) == per_block - 1))
        def _():
            block = lax.div(chunk, per_block)
            out_stage[block] = result[at_block(block)].T
            store(block).start()

        def settle(chunk):
            for piece in range(PIECES):
                @pl.when((core == 1) & (z < CHIPS - 1))
                def _():
                    carry(chunk, piece).wait_send()

                @pl.when((core == 1) & (z > 0))
                def _():
                    pass_on(chunk, piece).wait_send()

        @pl.when((chunk >= 1) & (chunk < N))
        def _():
            settle(chunk - 1)

        @pl.when(chunk == N - 1)
        def _():
            settle(chunk)

        return 0

    lax.fori_loop(0, N + LEVELS + z, step, 0)

    @pl.when(core == 0)
    def _():
        operator_copy.wait_send()

    for block in range(blocks):
        store(block).wait()


def hand_over(given, out, stage, in_sem, out_sem):
    parts = stage.shape[0]

    def move_in(part):
        return pltpu.make_async_copy(
            given.at[pl.ds(part * (F // parts), F // parts)], stage.at[part], in_sem.at[part]
        )

    def move_out(part):
        return pltpu.make_async_copy(
            stage.at[part], out.at[pl.ds(part * (F // parts), F // parts)], out_sem.at[part]
        )

    for part in range(parts):
        move_in(part).start()
    for part in range(parts):
        move_in(part).wait()
        move_out(part).start()
    for part in range(parts):
        move_out(part).wait()


def per_device(sources, merge_ops, sweep_ops):
    anywhere = pl.BlockSpec(memory_space=pl.ANY)
    dma = pltpu.SemaphoreType.DMA
    whole = pltpu.VMEM((COLS, F), F32)
    square = pltpu.VMEM((F, F), F32)
    blocks = COLS // BLOCK
    interface = pl.pallas_call(
        kernel,
        out_shape=jax.ShapeDtypeStruct((F, COLS), F32),
        in_specs=[anywhere] * 3,
        out_specs=anywhere,
        scratch_shapes=[
            pltpu.VMEM((blocks, F, BLOCK), F32),
            pltpu.VMEM((LEVELS, F, 2 * F), F32),
            square,
            square,
            square,
            pltpu.VMEM((LEVELS + 1, COLS, F), F32),
            pltpu.VMEM((LEVELS, COLS, F), F32),
            whole,
            whole,
            whole,
            pltpu.VMEM((blocks, F, BLOCK), F32),
            pltpu.VMEM((LEVELS, 2 * F, F), BF16),
            pltpu.VMEM((LEVELS, 2 * F, F), BF16),
            pltpu.VMEM((2 * F, F), BF16),
            pltpu.VMEM((2 * F, F), BF16),
            dma((blocks + LEVELS + 1,)),
            dma((LEVELS, N)),
            dma((LEVELS, N)),
            dma((N,)),
            dma((N,)),
            dma,
            dma,
            dma((PIECES, N)),
            dma((PIECES, N)),
            dma((PIECES, N)),
            dma((PIECES, N)),
            dma((blocks,)),
        ],
        compiler_params=pltpu.CompilerParams(
            collective_id=0, has_side_effects=True, vmem_limit_bytes=60 << 20
        ),
        cost_estimate=pl.CostEstimate(
            flops=3 * 10 * F * F * COLS, bytes_accessed=15 << 20, transcendentals=0
        ),
        name="solve",
    )(sources, merge_ops, sweep_ops)
    interface = pl.pallas_call(
        hand_over,
        out_shape=jax.ShapeDtypeStruct((F, COLS), F32),
        in_specs=[anywhere],
        out_specs=anywhere,
        scratch_shapes=[pltpu.VMEM((PARTS, F // PARTS, COLS), F32), dma((PARTS,)), dma((PARTS,))],
        name="hand_over",
    )(interface)
    return interface[None, None]


def solution(mesh):
    in_specs = (
        P("slab", "leaf", None, None),
        P(None, "slab", "leaf", None, None),
        P("slab", "leaf", None, None),
    )
    out_specs = P("slab", "leaf", None, None)
    return jax.shard_map(
        per_device, mesh=mesh, in_specs=in_specs, out_specs=out_specs, check_vma=False
    )
```

time: 131 us -> 127 us (0.969)
  local copies, waits for them, and re-layouts: 3.16 us -> 0 us
  Pallas kernels: 128 us -> 126 us
    pallas_call x1, Pallas kernels: 128 us -> 124 us  [per_device(): pl.pallas_call(kernel, out_shape=jax.ShapeDtypeStruct((F, COLS), F32), in...]
    unnamed x1 -> x0, local copies, waits for them, and re-layouts: 3.16 us -> none
    pallas_call x0 -> x1, Pallas kernels: none -> 2.42 us  [per_device(): pl.pallas_call(hand_over, out_shape=jax.ShapeDtypeStruct((F, COLS), F32),...]
where the time goes in v2:
time: 127 us; the launch traced here: 126 us
  Pallas kernels  126 us (99%)
    pallas_call x1, Pallas kernels, per_device(): pl.pallas_call(kernel, out_shape=jax.ShapeDtypeStruct((F, COLS), F32), in...  124 us

profile of v2, /device:TPU:96, one launch (start us, length us, event | category | flops | bytes accessed | tf_op | source)
XLA Modules:
  0.0 126.5 jit_solution(17967715417049851286)
XLA Ops:
  0.0 124.1 %solve.1.given = f32[512,1024]{1,0:T(8,128)} custom-call(f32[1,1,512,1024]{3,2,1,0:T(8,128)} %src.1, f32[4,1,1,512,1024]{4,3,2,1,0:T(8,128)} %merge.1, f32[1,1,512,512]{3,2,1,0:T(8,128)} %sweep.1), custom_call_target="tpu_custom_call" | custom-call | flops 8053063680 | bytes 15728640 | tf_op jit(solution)/shard_map/solve/pallas_call | solution.py:367
  124.1 2.4 %hand_over.1 = f32[512,1024]{1,0:T(8,128)} custom-call(f32[512,1024]{1,0:T(8,128)} %solve.1.given), custom_call_target="tpu_custom_call" | custom-call | tf_op jit(solution)/shard_map/hand_over/pallas_call | solution.py:409

commit v3 on v2

--- a/solution.py
+++ b/solution.py
@@ -20,7 +20,6 @@
 AHEAD = 2
 PIECES = 2
 PIECE = C // PIECES
-PARTS = 4
 
 
 def halves(value):
@@ -336,28 +335,6 @@
         store(block).wait()
 
 
-def hand_over(given, out, stage, in_sem, out_sem):
-    parts = stage.shape[0]
-
-    def move_in(part):
-        return pltpu.make_async_copy(
-            given.at[pl.ds(part * (F // parts), F // parts)], stage.at[part], in_sem.at[part]
-        )
-
-    def move_out(part):
-        return pltpu.make_async_copy(
-            stage.at[part], out.at[pl.ds(part * (F // parts), F // parts)], out_sem.at[part]
-        )
-
-    for part in range(parts):
-        move_in(part).start()
-    for part in range(parts):
-        move_in(part).wait()
-        move_out(part).start()
-    for part in range(parts):
-        move_out(part).wait()
-
-
 def per_device(sources, merge_ops, sweep_ops):
     anywhere = pl.BlockSpec(memory_space=pl.ANY)
     dma = pltpu.SemaphoreType.DMA
@@ -367,7 +344,7 @@
     interface = pl.pallas_call(
         kernel,
         out_shape=jax.ShapeDtypeStruct((F, COLS), F32),
-        in_specs=[anywhere] * 3,
+        in_specs=[pl.BlockSpec(memory_space=pltpu.HBM)] * 3,
         out_specs=anywhere,
         scratch_shapes=[
             pltpu.VMEM((blocks, F, BLOCK), F32),
@@ -399,21 +376,13 @@
             dma((blocks,)),
         ],
         compiler_params=pltpu.CompilerParams(
-            collective_id=0, has_side_effects=True, vmem_limit_bytes=60 << 20
+            collective_id=0, has_side_effects=True, vmem_limit_bytes=50 << 20
         ),
         cost_estimate=pl.CostEstimate(
             flops=3 * 10 * F * F * COLS, bytes_accessed=15 << 20, transcendentals=0
         ),
         name="solve",
-    )(sources, merge_ops, sweep_ops)
-    interface = pl.pallas_call(
-        hand_over,
-        out_shape=jax.ShapeDtypeStruct((F, COLS), F32),
-        in_specs=[anywhere],
-        out_specs=anywhere,
-        scratch_shapes=[pltpu.VMEM((PARTS, F // PARTS, COLS), F32), dma((PARTS,)), dma((PARTS,))],
-        name="hand_over",
-    )(interface)
+    )(*(pltpu.with_memory_space_constraint(each, pltpu.HBM) for each in (sources, merge_ops, sweep_ops)))
     return interface[None, None]
 
 

time: 127 us -> 125 us (0.984)
  Pallas kernels: 126 us -> 123 us
  local copies, waits for them, and re-layouts: 0 us -> 1.32 us
    pallas_call x1 -> x0, Pallas kernels: 2.42 us -> none  [per_device(): pl.pallas_call(hand_over, out_shape=jax.ShapeDtypeStruct((F, COLS), F32),...]
    unnamed x0 -> x1, local copies, waits for them, and re-layouts: none -> 1.32 us
where the time goes in v3:
time: 125 us
  Pallas kernels  123 us (98%)
  local copies, waits for them, and re-layouts  1.32 us (1%)
    pallas_call x1, Pallas kernels, per_device(): pl.pallas_call(kernel, out_shape=jax.ShapeDtypeStruct((F, COLS), F32), in...  123 us

profile of v3, /device:TPU:96, one launch (start us, length us, event | category | flops | bytes accessed | tf_op | source)
XLA Modules:
  0.0 124.7 jit_solution(5284714213871050592)
XLA Ops:
  0.0 123.4 %solve.1 = f32[512,1024]{1,0:T(8,128)S(1)} custom-call(f32[1,1,512,1024]{3,2,1,0:T(8,128)} %src.1, f32[4,1,1,512,1024]{4,3,2,1,0:T(8,128)} %merge.1, f32[1,1,512,512]{3,2,1,0:T(8,128)} %sweep.1), custom_call_target="tpu_custom_call" | custom-call | flops 8053063680 | bytes 15728640 | tf_op jit(solution)/shard_map/solve/pallas_call | solution.py:344
  123.4 1.3 %copy.5 = f32[1,1,512,1024]{3,2,1,0:T(8,128)} copy(f32[1,1,512,1024]{3,2,1,0:T(8,128)S(1)} %bitcast.1) | data formatting | bytes 4194304

commit v4 on v3

--- a/solution.py
+++ b/solution.py
@@ -55,6 +55,7 @@
         (slab, lax.rem(y + 2, 4) * 4 + x),
     )
     sibling = (slab + 1 - 2 * core, leaf)
+    late = 1 - core
     blocks = COLS // BLOCK
     per_block = BLOCK // C
 
@@ -225,7 +226,7 @@
             turn_source(lax.div(ahead, per_block))
 
         for level in range(LEVELS):
-            chunk = k - level
+            chunk = k - level - late * (level // (LEVELS - 1))
 
             @pl.when((chunk >= 0) & (chunk < N))
             def _():
@@ -251,7 +252,7 @@
                 def _():
                     exchange(0, ahead).start()
 
-        chunk = k - LEVELS
+        chunk = k - LEVELS - late
 
         @pl.when((chunk >= 0) & (chunk < N))
         def _():
@@ -277,7 +278,7 @@
             def _():
                 to_odd(chunk).wait_send()
 
-        chunk = k - LEVELS - z
+        chunk = k - LEVELS - late - z
         inside = (chunk >= 0) & (chunk < N)
 
         @pl.when(inside & (z > 0))
@@ -325,7 +326,7 @@
 
         return 0
 
-    lax.fori_loop(0, N + LEVELS + z, step, 0)
+    lax.fori_loop(0, N + LEVELS + late + z, step, 0)
 
     @pl.when(core == 0)
     def _():

time: 125 us -> 124 us (level)
  no operation moved by 1% of the time
where the time goes in v4:
time: 124 us
  Pallas kernels  123 us (99%)
  local copies, waits for them, and re-layouts  1.32 us (1%)
    pallas_call x1, Pallas kernels, per_device(): pl.pallas_call(kernel, out_shape=jax.ShapeDtypeStruct((F, COLS), F32), in...  123 us

profile of v4, /device:TPU:96, one launch (start us, length us, event | category | flops | bytes accessed | tf_op | source)
XLA Modules:
  0.0 123.9 jit_solution(16084717217195767222)
XLA Ops:
  0.0 122.6 %solve.1 = f32[512,1024]{1,0:T(8,128)S(1)} custom-call(f32[1,1,512,1024]{3,2,1,0:T(8,128)} %src.1, f32[4,1,1,512,1024]{4,3,2,1,0:T(8,128)} %merge.1, f32[1,1,512,512]{3,2,1,0:T(8,128)} %sweep.1), custom_call_target="tpu_custom_call" | custom-call | flops 8053063680 | bytes 15728640 | tf_op jit(solution)/shard_map/solve/pallas_call | solution.py:345
  122.6 1.3 %copy.5 = f32[1,1,512,1024]{3,2,1,0:T(8,128)} copy(f32[1,1,512,1024]{3,2,1,0:T(8,128)S(1)} %bitcast.1) | data formatting | bytes 4194304

commit v5 on v4

--- a/solution.py
+++ b/solution.py
@@ -39,10 +39,10 @@
 def kernel(
     src, merge, sweep, out,
     src_stage, merge_stage, sweep_stage, sweep_turned, even_turned,
-    state, arrived, from_even, carried, result, out_stage,
+    state, arrived, from_even, carried, result,
     merge_high, merge_low, sweep_high, sweep_low,
     load_sem, send_sem, recv_sem, even_send, even_recv, op_send, op_recv,
-    carry_send, carry_recv, pass_send, pass_recv, store_sem,
+    carry_send, carry_recv, pass_send, pass_recv,
 ):
     slab = lax.axis_index("slab")
     leaf = lax.axis_index("leaf")
@@ -76,6 +76,14 @@
         sweep.at[0, 0], sweep_stage, load_sem.at[blocks + LEVELS]
     )
 
+    barrier = pltpu.get_barrier_semaphore()
+    for device in (partner[3], partner[1], partner[2], partner[0], sibling):
+        pl.semaphore_signal(barrier, inc=1, device_id=device, device_id_type=MESH)
+
+    @pl.when((z > 0) & (core == 1))
+    def _():
+        pl.semaphore_signal(barrier, inc=1, device_id=(slab - 2, leaf), device_id_type=MESH)
+
     load_source(0).start()
     load_merge(0).start()
     for block in range(1, blocks):
@@ -83,14 +91,6 @@
     for level in range(1, LEVELS):
         load_merge(level).start()
     load_sweep.start()
-
-    barrier = pltpu.get_barrier_semaphore()
-    for device in partner + (sibling,):
-        pl.semaphore_signal(barrier, inc=1, device_id=device, device_id_type=MESH)
-
-    @pl.when((z > 0) & (core == 1))
-    def _():
-        pl.semaphore_signal(barrier, inc=1, device_id=(slab - 2, leaf), device_id_type=MESH)
 
     last = lax.div(z + 1, CHIPS)
     pl.semaphore_wait(barrier, 5 + core * (1 - last))
@@ -148,11 +148,6 @@
             recv_sem=pass_recv.at[piece, chunk],
             device_id=sibling,
             device_id_type=MESH,
-        )
-
-    def store(block):
-        return pltpu.make_async_copy(
-            out_stage.at[block], out.at[:, at_block(block)], store_sem.at[block]
         )
 
     def turn_source(block):
@@ -303,8 +298,7 @@
         @pl.when(inside & (lax.rem(chunk, per_block) == per_block - 1))
         def _():
             block = lax.div(chunk, per_block)
-            out_stage[block] = result[at_block(block)].T
-            store(block).start()
+            out[:, at_block(block)] = result[at_block(block)].T
 
         def settle(chunk):
             for piece in range(PIECES):
@@ -331,9 +325,6 @@
     @pl.when(core == 0)
     def _():
         operator_copy.wait_send()
-
-    for block in range(blocks):
-        store(block).wait()
 
 
 def per_device(sources, merge_ops, sweep_ops):
@@ -346,7 +337,7 @@
         kernel,
         out_shape=jax.ShapeDtypeStruct((F, COLS), F32),
         in_specs=[pl.BlockSpec(memory_space=pltpu.HBM)] * 3,
-        out_specs=anywhere,
+        out_specs=pl.BlockSpec(memory_space=pltpu.VMEM),
         scratch_shapes=[
             pltpu.VMEM((blocks, F, BLOCK), F32),
             pltpu.VMEM((LEVELS, F, 2 * F), F32),
@@ -358,7 +349,6 @@
             whole,
             whole,
             whole,
-            pltpu.VMEM((blocks, F, BLOCK), F32),
             pltpu.VMEM((LEVELS, 2 * F, F), BF16),
             pltpu.VMEM((LEVELS, 2 * F, F), BF16),
             pltpu.VMEM((2 * F, F), BF16),
@@ -374,7 +364,6 @@
             dma((PIECES, N)),
             dma((PIECES, N)),
             dma((PIECES, N)),
-            dma((blocks,)),
         ],
         compiler_params=pltpu.CompilerParams(
             collective_id=0, has_side_effects=True, vmem_limit_bytes=50 << 20

time: 124 us -> 124 us (level)
  no operation moved by 1% of the time
where the time goes in v5:
time: 124 us
  Pallas kernels  122 us (98%)
  local copies, waits for them, and re-layouts  1.32 us (1%)
    pallas_call x1, Pallas kernels, per_device(): pl.pallas_call(kernel, out_shape=jax.ShapeDtypeStruct((F, COLS), F32), in...  122 us

profile of v5, /device:TPU:96, one launch (start us, length us, event | category | flops | bytes accessed | tf_op | source)
XLA Modules:
  0.0 123.7 jit_solution(2836390800246267103)
XLA Ops:
  0.0 122.3 %solve.1 = f32[512,1024]{1,0:T(8,128)S(1)} custom-call(f32[1,1,512,1024]{3,2,1,0:T(8,128)} %src.1, f32[4,1,1,512,1024]{4,3,2,1,0:T(8,128)} %merge.1, f32[1,1,512,512]{3,2,1,0:T(8,128)} %sweep.1), custom_call_target="tpu_custom_call" | custom-call | flops 8053063680 | bytes 15728640 | tf_op jit(solution)/shard_map/solve/pallas_call | solution.py:336
  122.3 1.3 %copy.5 = f32[1,1,512,1024]{3,2,1,0:T(8,128)} copy(f32[1,1,512,1024]{3,2,1,0:T(8,128)S(1)} %bitcast.1) | data formatting | bytes 4194304
